TPU v7x, 32 devices: a whole 2x2x4 slice. The times are simulated.
32 devices in a mesh: groups: 2 (over y), seq: 4 (over z), section: 2 (over x), chan: 2 (over core).
Axes of the slice: x: 2, y: 2, z: 4, core: 2. Of those that a mesh axis runs over, the one named last changes fastest.
Arguments:
- base_codes: int32 [131072], P(('groups', 'seq', 'section')), parts along dimension 0, may hold values from 0 to 3
- stem_weight: bfloat16 [64, 768], replicated, as said below
- conv_gain: float32 [768], replicated, may hold values from 0.1 to 1.9
- dilated_conv_weight: bfloat16 [3, 768, 768], P(None, None, 'chan'), may hold values from -0.125 to 0.125
- widen_weight: bfloat16 [768, 1536], P(None, 'chan'), may hold values from -0.21875 to 0.21875
- token_gain: float32 [1536], replicated, may hold values from 0.1 to 1.9
- proj_weight: bfloat16 [1536, 256], replicated, may hold values from -0.15625 to 0.15625
- dist_weight: float32 [128], replicated, may hold values from -4 to 4
- pair_weight_one: bfloat16 [3, 3, 128, 128], P(None, None, None, 'chan'), may hold values from -0.1875 to 0.1875
- pair_weight_two: bfloat16 [3, 3, 128, 128], P(None, None, None, 'chan'), may hold values from -0.1875 to 0.1875
Outputs:
- fine_features: bfloat16 [4096, 1536], P(('groups', 'seq', 'section'), 'chan'), parts along dimension 0
- pair_map: bfloat16 [128, 64, 32], P('chan', ('groups', 'seq'), 'section'), parts along dimension 1
There are 2 independent parts, one for each index of `groups`. A program takes and returns all parts, laid end to end along the dimension named above; an argument that names none is the same for every part. Nothing has to cross between parts.
Inputs may be any that keep to these rules, and one draw needn't show every extreme that they name: Each entry of stem_weight is under 9 / sqrt(16) in magnitude.
All inputs are finite; a program needn't handle non-finite values.
Results may differ from a plain program's by a relative error of at most 0.015.
Values may be sent and summed in bfloat16 or wider, within the bound.
No kernel may reach another device: no remote copies, remote signals or barrier semaphores. Data moves between devices by JAX's collectives and lax.ppermute only.
A program may use at most 64 MiB of HBM per device.

v0:
```python
import math
import jax
import jax.numpy as jnp
from jax import lax
from jax.sharding import PartitionSpec as P

PC = 128
PATCH = 16
POOL = 64
DILATION_ROWS = 4
epsilon = 1e-06


def padded(cells, sides, width):
    for axis, dim in sides:
        count = lax.axis_size(axis)
        ends = count - 1
        head = lax.slice_in_dim(cells, 0, width, axis=dim)
        tail = lax.slice_in_dim(cells, cells.shape[dim] - width, cells.shape[dim], axis=dim)
        cells = jnp.concatenate(
            [
                lax.ppermute(tail, axis, [(i, (i + 1) % count) for i in range(ends)]),
                cells,
                lax.ppermute(head, axis, [((i + 1) % count, i) for i in range(ends)]),
            ],
            axis=dim,
        )
    return cells


def row_norm(values, gain):
    mean_square = jnp.mean(values * values, axis=1, keepdims=True)
    return values * lax.rsqrt(mean_square + epsilon) * gain


def pair_conv(active, weight):
    row_len = active.shape[1] - 2
    col_len = active.shape[2] - 2
    total = jnp.zeros((weight.shape[3], row_len, col_len), jnp.float32)
    for shift_row in range(3):
        for shift_col in range(3):
            window = active[:, shift_row : shift_row + row_len, shift_col : shift_col + col_len]
            total = total + jnp.einsum(
                "co,crs->ors",
                weight[shift_row, shift_col],
                window,
                preferred_element_type=jnp.float32,
            )
    return total


def make_pair(row_factor, col_factor, row_index, col_index, dist_weight, tokens_total):
    gap = jnp.abs(row_index[:, None] - col_index[None, :]).astype(jnp.float32)
    distance = jnp.log1p(gap) / math.log(tokens_total)
    product = (
        row_factor.astype(jnp.float32).T[:, :, None] * col_factor.astype(jnp.float32).T[:, None, :]
    )
    return product + dist_weight[:, None, None] * distance[None, :, :]


def per_device(
    base_codes,
    stem_weight,
    conv_gain,
    dilated_conv_weight,
    widen_weight,
    token_gain,
    proj_weight,
    dist_weight,
    pair_weight_one,
    pair_weight_two,
):
    count_of_rows = base_codes.shape[0] // PATCH
    coded = base_codes.reshape(count_of_rows, PATCH)
    onehot = (
        (coded[:, :, None] == jnp.arange(4, dtype=jnp.int32)[None, None, :])
        .astype(jnp.bfloat16)
        .reshape(count_of_rows, 4 * PATCH)
    )
    half_width = dilated_conv_weight.shape[2]
    own_index = lax.axis_index("chan")
    weight_own = lax.dynamic_slice_in_dim(stem_weight, own_index * half_width, half_width, 1)
    stem_own = jnp.dot(onehot, weight_own, preferred_element_type=jnp.float32).astype(jnp.bfloat16)
    full_stem_output = lax.all_gather(stem_own, "chan", axis=1, tiled=True)
    padded_rows = padded(full_stem_output, ((("seq", "section"), 0),), DILATION_ROWS)
    normalized_rows = row_norm(padded_rows.astype(jnp.float32), conv_gain).astype(jnp.bfloat16)
    summed_taps = jnp.zeros((count_of_rows, half_width), jnp.float32)
    for row_shift_amount in range(3):
        summed_taps = summed_taps + jnp.dot(
            normalized_rows[
                row_shift_amount * DILATION_ROWS : row_shift_amount * DILATION_ROWS + count_of_rows
            ],
            dilated_conv_weight[row_shift_amount],
            preferred_element_type=jnp.float32,
        )
    tower = (stem_own.astype(jnp.float32) + jax.nn.gelu(summed_taps)).astype(jnp.bfloat16)
    halved = jnp.maximum(tower[0::2], tower[1::2])
    widened = jnp.dot(
        lax.all_gather(halved, "chan", axis=1, tiled=True),
        widen_weight,
        preferred_element_type=jnp.float32,
    )
    fine_features = jax.nn.gelu(widened).astype(jnp.bfloat16)
    tok_count = fine_features.shape[0] // POOL
    token = jnp.mean(
        fine_features.astype(jnp.float32).reshape(tok_count, POOL, fine_features.shape[1]), axis=1
    ).astype(jnp.bfloat16)
    token_full = lax.all_gather(token, "chan", axis=1, tiled=True)
    token_norm = row_norm(token_full.astype(jnp.float32), token_gain).astype(jnp.bfloat16)
    factors = jnp.dot(token_norm, proj_weight, preferred_element_type=jnp.float32).astype(
        jnp.bfloat16
    )
    seq_count = lax.axis_size("seq")
    section_count = lax.axis_size("section")
    tokens_total = tok_count * seq_count * section_count
    tile_height = tok_count * section_count
    tile_width = tok_count * seq_count
    row_anchor = lax.axis_index("seq") * tile_height
    col_anchor = lax.axis_index("section") * tile_width
    pair_own = pair_weight_one.shape[3]
    every_token = lax.all_gather(factors, ("seq", "section"), axis=0, tiled=True)
    zero_padded = jnp.pad(every_token, ((1, 1), (0, 0)))
    row_factor = lax.dynamic_slice_in_dim(zero_padded, row_anchor, tile_height + 2, 0)[:, :PC]
    col_factor = lax.dynamic_slice_in_dim(zero_padded, col_anchor, tile_width + 2, 0)[:, PC:]
    row_index = row_anchor - 1 + jnp.arange(tile_height + 2, dtype=jnp.int32)
    col_index = col_anchor - 1 + jnp.arange(tile_width + 2, dtype=jnp.int32)
    extended = make_pair(
        row_factor, col_factor, row_index, col_index, dist_weight, tokens_total
    ).astype(jnp.bfloat16)
    row_valid = (row_index >= 0) & (row_index < tokens_total)
    col_valid = (col_index >= 0) & (col_index < tokens_total)
    inside = row_valid[:, None] & col_valid[None, :]
    act_one = jnp.where(inside[None, :, :], jax.nn.gelu(extended.astype(jnp.float32)), 0.0).astype(
        jnp.bfloat16
    )
    pair_start = extended[:, 1:-1, 1:-1]
    start_own = lax.dynamic_slice_in_dim(pair_start, own_index * pair_own, pair_own, 0)
    pair_mid = (start_own.astype(jnp.float32) + pair_conv(act_one, pair_weight_one)).astype(
        jnp.bfloat16
    )
    mid_full = lax.all_gather(pair_mid, "chan", axis=0, tiled=True)
    act_local_two = jax.nn.gelu(mid_full.astype(jnp.float32)).astype(jnp.bfloat16)
    act_two = padded(act_local_two, (("seq", 1), ("section", 2)), 1)
    pair_map = (pair_mid.astype(jnp.float32) + pair_conv(act_two, pair_weight_two)).astype(
        jnp.bfloat16
    )
    return (fine_features, pair_map)


def solution(mesh):
    in_specs = (
        P(("groups", "seq", "section")),
        P(),
        P(),
        P(None, None, "chan"),
        P(None, "chan"),
        P(),
        P(),
        P(),
        P(None, None, None, "chan"),
        P(None, None, None, "chan"),
    )
    out_specs = (P(("groups", "seq", "section"), "chan"), P("chan", ("groups", "seq"), "section"))
    return jax.shard_map(
        per_device, mesh=mesh, in_specs=in_specs, out_specs=out_specs, check_vma=False
    )
```

profile of v0, /device:TPU:0, one launch (start us, length us, event | category | flops | bytes accessed | tf_op | source)
XLA Modules:
  0.0 73.8 jit_solution(9603304205572424095)
XLA Ops:
  0.7 1.0 %eq.22 = s32[512,16]{1,0:T(8,128)S(1)} reshape(s32[8192]{0:T(1024)} %param.10) | data formatting | bytes 65536 | tf_op jit(solution)/shard_map/eq | solution.py:76
  1.9 1.2 %convolution_convert_fusion = bf16[512,384]{1,0:T(8,128)(2,1)S(1)} fusion(s32[512,64]{0,1:T(8,128)S(1)} %eq.24, s32[64]{0:T(128)S(1)} %eq.26, bf16[64,768]{1,0:T(8,128)(2,1)} %param.11, s32[]{:T(128)S(6)} %select_n.16), kind=kOutput, calls=%fused_computation.7 | convolution fusion | flops 25395200 | bytes 573700 | tf_op jit(solution)/shard_map/dot_general | solution.py:83
  3.1 2.5 %all_gather.15 = bf16[512,768]{1,0:T(8,128)(2,1)S(1)} all-gather(bf16[512,384]{1,0:T(8,128)(2,1)S(1)} %convolution_convert_fusion), channel_id=1, replica_groups=mesh['groups'=2,'seq'=4,'section'=2,'chan'=2] {'chan'}, dimensions={1}, use_global_device_ids=true | all-gather | bytes 1179648 | tf_op jit(solution)/shard_map/all_gather | solution.py:84
  5.6 4.8 %collective-permute-start = (bf16[4,768]{1,0:T(4,128)(2,1)S(1)}, bf16[4,768]{1,0:T(4,128)(2,1)S(1)}, u32[]{:S(2)}, u32[]{:S(2)}) collective-permute-start(bf16[4,768]{1,0:T(4,128)(2,1)S(1)} %get-tuple-element.4), channel_id=1, source_target_pairs={{0,2},{2,4},{4,6},{6,8},{8,10},{10,12},{12,14},{1,3},{3,5},{5,7},{... | collective-permute-start | bytes 18440 | tf_op jit(solution)/shard_map/ppermute | solution.py:22
  10.4 1.3 %collective-permute-start.1 = (bf16[4,768]{1,0:T(4,128)(2,1)S(1)}, bf16[4,768]{1,0:T(4,128)(2,1)S(1)}, u32[]{:S(2)}, u32[]{:S(2)}) collective-permute-start(bf16[4,768]{1,0:T(4,128)(2,1)S(1)} %get-tuple-element.5), channel_id=1, source_target_pairs={{2,0},{4,2},{6,4},{8,6},{10,8},{12,10},{14,12},{3,1},{5,3},{7,5},{... | collective-permute-start | bytes 18440 | tf_op jit(solution)/shard_map/ppermute | solution.py:24
  11.9 4.0 %collective-permute-done.1 = bf16[4,768]{1,0:T(4,128)(2,1)S(1)} collective-permute-done((bf16[4,768]{1,0:T(4,128)(2,1)S(1)}, bf16[4,768]{1,0:T(4,128)(2,1)S(1)}, u32[]{:S(2)}, u32[]{:S(2)}) %collective-permute-start.1) | collective-permute-done | bytes 6176 | tf_op jit(solution)/shard_map/ppermute | solution.py:24
  15.9 0.3 fusion
  16.6 0.6 fusion.34
  17.2 0.6 convolution_add_fusion.1
  17.8 0.8 %fusion.24 = bf16[512,384]{1,0:T(8,128)(2,1)S(1)} fusion(f32[512,384]{1,0:T(8,128)S(1)} %convolution_add_fusion.1, bf16[520,768]{1,0:T(8,128)(2,1)S(1)} %fusion.2, bf16[512,384]{1,0:T(8,128)(2,1)S(1)} %convolution_convert_fusion, bf16[3,768,384]{2,1,0:T(8,128)(2,1)S(1)} %copy-done.2), kind=kOutput, calls=%fused_computation.43 | convolution fusion | flops 304349184 | bytes 2949120 | tf_op jit(solution)/shard_map/dot_general | solution.py:89
  18.6 0.6 slice.172
  19.2 0.6 slice.173
  19.8 2.1 %all_gather.16 = bf16[256,768]{1,0:T(8,128)(2,1)S(1)} all-gather(bf16[256,384]{1,0:T(8,128)(2,1)S(1)} %max.3), channel_id=1, replica_groups=mesh['groups'=2,'seq'=4,'section'=2,'chan'=2] {'chan'}, dimensions={1}, use_global_device_ids=true | all-gather | bytes 589824 | tf_op jit(solution)/shard_map/all_gather | solution.py:99
  21.9 1.4 %convert_reduce_fusion = (f32[4,768]{1,0:T(4,128)S(1)}, bf16[256,768]{1,0:T(8,128)(2,1)}) fusion(bf16[256,768]{1,0:T(8,128)(2,1)S(1)} %all_gather.16, bf16[768,768]{1,0:T(8,128)(2,1)S(1)} %copy-done), kind=kOutput, calls=%fused_computation.56 | convolution fusion | flops 304149504 | bytes 1978368 | tf_op jit(solution)/shard_map/dot_general | solution.py:98
  23.3 1.8 %all_gather.17 = bf16[4,1536]{1,0:T(4,128)(2,1)S(1)} all-gather(bf16[4,768]{1,0:T(4,128)(2,1)S(1)} %multiply_convert_fusion), channel_id=1, replica_groups=mesh['groups'=2,'seq'=4,'section'=2,'chan'=2] {'chan'}, dimensions={1}, use_global_device_ids=true | all-gather | bytes 18432 | tf_op jit(solution)/shard_map/all_gather | solution.py:108
  25.5 26.6 %all-gather = bf16[8,4,256]{2,1,0:T(4,128)(2,1)S(1)} all-gather(bf16[1,4,256]{2,1,0:T(4,128)(2,1)S(1)} %fusion.15), channel_id=1, replica_groups=mesh['groups'=2,'seq'=4,'section'=2,'chan'=2] {'seq','section'}, dimensions={0}, use_global_device_ids=true | all-gather | bytes 18432 | tf_op jit(solution)/shard_map/all_gather | solution.py:121
  53.8 2.0 %all_gather.19 = bf16[128,8,16]{2,1,0:T(8,128)(2,1)S(1)} all-gather(bf16[64,8,16]{2,1,0:T(8,128)(2,1)S(1)} %copy.17), channel_id=1, replica_groups=mesh['groups'=2,'seq'=4,'section'=2,'chan'=2] {'chan'}, dimensions={0}, use_global_device_ids=true | all-gather | bytes 49152 | tf_op jit(solution)/shard_map/all_gather | solution.py:141
  56.1 2.2 %collective-permute-start.2 = (bf16[128,1,16]{0,2,1:T(8,128)(2,1)S(1)}, bf16[128,1,16]{0,2,1:T(8,128)(2,1)S(1)}, u32[]{:S(2)}, u32[]{:S(2)}) collective-permute-start(bf16[128,1,16]{0,2,1:T(8,128)(2,1)S(1)} %get-tuple-element.10), channel_id=1, source_target_pairs={{0,4},{4,8},{8,12},{1,5},{5,9},{9,13},{2,6},{6,10},{10,14},{3,7},{... | collective-permute-start | bytes 12296 | tf_op jit(solution)/shard_map/ppermute | solution.py:22
  58.3 1.3 %collective-permute-start.3 = (bf16[128,1,16]{0,2,1:T(8,128)(2,1)S(1)}, bf16[128,1,16]{0,2,1:T(8,128)(2,1)S(1)}, u32[]{:S(2)}, u32[]{:S(2)}) collective-permute-start(bf16[128,1,16]{0,2,1:T(8,128)(2,1)S(1)} %get-tuple-element.11), channel_id=1, source_target_pairs={{4,0},{8,4},{12,8},{5,1},{9,5},{13,9},{6,2},{10,6},{14,10},{7,3},{... | collective-permute-start | bytes 12296 | tf_op jit(solution)/shard_map/ppermute | solution.py:24
  59.7 4.0 %collective-permute-done.3 = bf16[128,1,16]{0,2,1:T(8,128)(2,1)S(1)} collective-permute-done((bf16[128,1,16]{0,2,1:T(8,128)(2,1)S(1)}, bf16[128,1,16]{0,2,1:T(8,128)(2,1)S(1)}, u32[]{:S(2)}, u32[]{:S(2)}) %collective-permute-start.3) | collective-permute-done | bytes 4128 | tf_op jit(solution)/shard_map/ppermute | solution.py:24
  63.8 3.0 %collective-permute-start.4 = (bf16[128,10,1]{0,2,1:T(2,128)(2,1)S(1)}, bf16[128,10,1]{0,2,1:T(2,128)(2,1)S(1)}, u32[]{:S(2)}, u32[]{:S(2)}) collective-permute-start(bf16[128,10,1]{0,2,1:T(2,128)(2,1)S(1)} %get-tuple-element.8), channel_id=1, source_target_pairs={{0,2},{1,3},{4,6},{5,7},{8,10},{9,11},{12,14},{13,15},{16,18},{17,... | collective-permute-start | bytes 7688 | tf_op jit(solution)/shard_map/ppermute | solution.py:22
  66.8 1.3 %collective-permute-start.5 = (bf16[128,10,1]{0,2,1:T(2,128)(2,1)S(1)}, bf16[128,10,1]{0,2,1:T(2,128)(2,1)S(1)}, u32[]{:S(2)}, u32[]{:S(2)}) collective-permute-start(bf16[128,10,1]{0,2,1:T(2,128)(2,1)S(1)} %get-tuple-element.9), channel_id=1, source_target_pairs={{2,0},{3,1},{6,4},{7,5},{10,8},{11,9},{14,12},{15,13},{18,16},{19,... | collective-permute-start | bytes 7688 | tf_op jit(solution)/shard_map/ppermute | solution.py:24
  68.4 4.0 %collective-permute-done.5 = bf16[128,10,1]{0,2,1:T(2,128)(2,1)S(1)} collective-permute-done((bf16[128,10,1]{0,2,1:T(2,128)(2,1)S(1)}, bf16[128,10,1]{0,2,1:T(2,128)(2,1)S(1)}, u32[]{:S(2)}, u32[]{:S(2)}) %collective-permute-start.5) | collective-permute-done | bytes 2592 | tf_op jit(solution)/shard_map/ppermute | solution.py:24
  73.1 0.8 %fusion.14 = bf16[64,8,16]{0,2,1:T(8,128)(2,1)} fusion(f32[8,16,64]{2,1,0:T(8,128)S(1)} %fusion.67, f32[8,16,64]{2,1,0:T(8,128)S(1)} %fusion.63, f32[8,16,64]{2,1,0:T(8,128)S(1)} %fusion.69, f32[8,16,64]{2,1,0:T(8,128)S(1)} %fusion.9, bf16[64,8,16]{0,2,1:T(8,128)(2,1)S(1)} %fusion.13, bf16[128,10,17]{0,2,1:T(8,128)(2,1)S(1)} %get-tuple-element.7, ...), kind=kOutput, calls=%fused_computation.31 | convolution fusion | flops 2154496 | bytes 360448 | tf_op jit(solution)/shard_map/co,crs->ors/dot_general | solution.py:43
  (66 shorter events, 4.3 us)
Async XLA Ops:
  0.6 21.3 %copy-start = (bf16[768,768]{1,0:T(8,128)(2,1)S(1)}, bf16[768,768]{1,0:T(8,128)(2,1)}, u32[]{:S(2)}) copy-start(bf16[768,768]{1,0:T(8,128)(2,1)} %param.14) | copy-start | bytes 3538948
  1.7 14.5 %copy-start.6 = (f32[768]{0:T(1024)S(1)}, f32[768]{0:T(1024)}, u32[]{:S(2)}) copy-start(f32[768]{0:T(1024)} %param.12) | copy-start | bytes 9220
  5.6 6.3 %collective-permute-start = (bf16[4,768]{1,0:T(4,128)(2,1)S(1)}, bf16[4,768]{1,0:T(4,128)(2,1)S(1)}, u32[]{:S(2)}, u32[]{:S(2)}) collective-permute-start(bf16[4,768]{1,0:T(4,128)(2,1)S(1)} %get-tuple-element.4), channel_id=1, source_target_pairs={{0,2},{2,4},{4,6},{6,8},{8,10},{10,12},{12,14},{1,3},{3,5},{5,7},{... | collective-permute-start | bytes 18440 | tf_op jit(solution)/shard_map/ppermute | solution.py:22
  10.4 5.5 %collective-permute-start.1 = (bf16[4,768]{1,0:T(4,128)(2,1)S(1)}, bf16[4,768]{1,0:T(4,128)(2,1)S(1)}, u32[]{:S(2)}, u32[]{:S(2)}) collective-permute-start(bf16[4,768]{1,0:T(4,128)(2,1)S(1)} %get-tuple-element.5), channel_id=1, source_target_pairs={{2,0},{4,2},{6,4},{8,6},{10,8},{12,10},{14,12},{3,1},{5,3},{7,5},{... | collective-permute-start | bytes 18440 | tf_op jit(solution)/shard_map/ppermute | solution.py:24
  11.9 4.7 %copy-start.2 = (bf16[3,768,384]{2,1,0:T(8,128)(2,1)S(1)}, bf16[3,768,384]{2,1,0:T(8,128)(2,1)}, u32[]{:S(2)}) copy-start(bf16[3,768,384]{2,1,0:T(8,128)(2,1)} %param.13) | copy-start | bytes 5308420
  21.9 3.3 %copy-start.1 = (bf16[1536,256]{1,0:T(8,128)(2,1)S(1)}, bf16[1536,256]{1,0:T(8,128)(2,1)}, u32[]{:S(2)}) copy-start(bf16[1536,256]{1,0:T(8,128)(2,1)} %param.16) | copy-start | bytes 2359300
  21.9 3.4 %copy-start.5 = (f32[1536]{0:T(1024)S(1)}, f32[1536]{0:T(1024)}, u32[]{:S(2)}) copy-start(f32[1536]{0:T(1024)} %param.15) | copy-start | bytes 18436
  21.9 30.3 %copy-start.7 = (f32[128]{0:T(128)S(1)}, f32[128]{0:T(128)}, u32[]{:S(2)}) copy-start(f32[128]{0:T(128)} %param.17) | copy-start | bytes 1540
  21.9 30.5 %copy-start.3 = (bf16[3,3,128,64]{2,3,1,0:T(8,128)(2,1)S(1)}, bf16[3,3,128,64]{2,3,1,0:T(8,128)(2,1)}, u32[]{:S(2)}) copy-start(bf16[3,3,128,64]{2,3,1,0:T(8,128)(2,1)} %param.18) | copy-start | bytes 442372
  25.5 34.0 %copy-start.4 = (bf16[3,3,128,64]{2,3,1,0:T(8,128)(2,1)S(1)}, bf16[3,3,128,64]{2,3,1,0:T(8,128)(2,1)}, u32[]{:S(2)}) copy-start(bf16[3,3,128,64]{2,3,1,0:T(8,128)(2,1)} %param.19) | copy-start | bytes 442372
  56.1 3.6 %collective-permute-start.2 = (bf16[128,1,16]{0,2,1:T(8,128)(2,1)S(1)}, bf16[128,1,16]{0,2,1:T(8,128)(2,1)S(1)}, u32[]{:S(2)}, u32[]{:S(2)}) collective-permute-start(bf16[128,1,16]{0,2,1:T(8,128)(2,1)S(1)} %get-tuple-element.10), channel_id=1, source_target_pairs={{0,4},{4,8},{8,12},{1,5},{5,9},{9,13},{2,6},{6,10},{10,14},{3,7},{... | collective-permute-start | bytes 12296 | tf_op jit(solution)/shard_map/ppermute | solution.py:22
  58.3 5.5 %collective-permute-start.3 = (bf16[128,1,16]{0,2,1:T(8,128)(2,1)S(1)}, bf16[128,1,16]{0,2,1:T(8,128)(2,1)S(1)}, u32[]{:S(2)}, u32[]{:S(2)}) collective-permute-start(bf16[128,1,16]{0,2,1:T(8,128)(2,1)S(1)} %get-tuple-element.11), channel_id=1, source_target_pairs={{4,0},{8,4},{12,8},{5,1},{9,5},{13,9},{6,2},{10,6},{14,10},{7,3},{... | collective-permute-start | bytes 12296 | tf_op jit(solution)/shard_map/ppermute | solution.py:24
  63.8 4.6 %collective-permute-start.4 = (bf16[128,10,1]{0,2,1:T(2,128)(2,1)S(1)}, bf16[128,10,1]{0,2,1:T(2,128)(2,1)S(1)}, u32[]{:S(2)}, u32[]{:S(2)}) collective-permute-start(bf16[128,10,1]{0,2,1:T(2,128)(2,1)S(1)} %get-tuple-element.8), channel_id=1, source_target_pairs={{0,2},{1,3},{4,6},{5,7},{8,10},{9,11},{12,14},{13,15},{16,18},{17,... | collective-permute-start | bytes 7688 | tf_op jit(solution)/shard_map/ppermute | solution.py:22
  66.8 5.5 %collective-permute-start.5 = (bf16[128,10,1]{0,2,1:T(2,128)(2,1)S(1)}, bf16[128,10,1]{0,2,1:T(2,128)(2,1)S(1)}, u32[]{:S(2)}, u32[]{:S(2)}) collective-permute-start(bf16[128,10,1]{0,2,1:T(2,128)(2,1)S(1)} %get-tuple-element.9), channel_id=1, source_target_pairs={{2,0},{3,1},{6,4},{7,5},{10,8},{11,9},{14,12},{15,13},{18,16},{19,... | collective-permute-start | bytes 7688 | tf_op jit(solution)/shard_map/ppermute | solution.py:24
where the time goes:
time: 74.2 us; the launch traced here: 73.8 us
  blocking collectives  35 us (47%)
  starting transfers between devices  13.8 us (19%)
  waiting for transfers between devices  12 us (16%)
  matrix products  7.84 us (11%)
  local copies, waits for them, and re-layouts  2.83 us (4%)
  other arithmetic  1.39 us (2%)
  between operations  0.97 us (1%)
    all_gather x1, blocking collectives, per_device(): lax.all_gather(factors, ('seq', 'section'), axis=0, tiled=True)  26.6 us
    ppermute x3, waiting for transfers between devices, padded(): lax.ppermute(head, axis, [((i + 1) % count, i) for i in range(ends)])  12 us
    ppermute x3, starting transfers between devices, padded(): lax.ppermute(tail, axis, [(i, (i + 1) % count) for i in range(ends)])  9.96 us
    ppermute x3, starting transfers between devices, padded(): lax.ppermute(head, axis, [((i + 1) % count, i) for i in range(ends)])  3.88 us
    dot_general x18, matrix products, pair_conv(): jnp.einsum('co,crs->ors', weight[shift_row, shift_col], window, preferred...  3.11 us
    all_gather x1, blocking collectives, per_device(): full_stem_output = lax.all_gather(stem_own, 'chan', axis=1, tiled=True)  2.49 us
    all_gather x1, blocking collectives, per_device(): lax.all_gather(halved, 'chan', axis=1, tiled=True)  2.09 us
    all_gather x1, blocking collectives, per_device(): mid_full = lax.all_gather(pair_mid, 'chan', axis=0, tiled=True)  1.99 us
  transfers between devices with their start and end apart: 6, of which 3 were waited for; matrix products, arithmetic and copies ran while one was open for 1% of the time, Pallas kernels for 0%

commit v1 on v0

--- a/solution.py
+++ b/solution.py
@@ -118,7 +118,18 @@
     row_anchor = lax.axis_index("seq") * tile_height
     col_anchor = lax.axis_index("section") * tile_width
     pair_own = pair_weight_one.shape[3]
-    every_token = lax.all_gather(factors, ("seq", "section"), axis=0, tiled=True)
+    ways = lax.axis_size(("seq", "section"))
+    up = [(d, (d + 1) % ways) for d in range(ways)]
+    down = [(d, (d - 1) % ways) for d in range(ways)]
+    earlier, later = ([factors], [factors])
+    for _ in range(ways // 2):
+        earlier.append(lax.ppermute(earlier[-1], ("seq", "section"), up))
+    for _ in range((ways - 1) // 2):
+        later.append(lax.ppermute(later[-1], ("seq", "section"), down))
+    line = jnp.concatenate([*earlier[::-1], *later[1:]], axis=0)
+    every_token = jnp.roll(
+        line, (lax.axis_index(("seq", "section")) - ways // 2) * factors.shape[0], axis=0
+    )
     zero_padded = jnp.pad(every_token, ((1, 1), (0, 0)))
     row_factor = lax.dynamic_slice_in_dim(zero_padded, row_anchor, tile_height + 2, 0)[:, :PC]
     col_factor = lax.dynamic_slice_in_dim(zero_padded, col_anchor, tile_width + 2, 0)[:, PC:]

time: 74.2 us -> 70.3 us (0.947)
  blocking collectives: 35 us -> 8.39 us
  starting transfers between devices: 13.8 us -> 25.4 us
  waiting for transfers between devices: 12 us -> 22.9 us
    all_gather x1 -> x0, blocking collectives: 26.6 us -> none  [per_device(): lax.all_gather(factors, ('seq', 'section'), axis=0, tiled=True)]
    ppermute x0 -> x7, starting transfers between devices: none -> 14.2 us  [the longest x3 11.8 us: per_device(): later.append(lax.ppermute(later[-1], ('seq', 'section'), down))]
    ppermute x0 -> x7, waiting for transfers between devices: none -> 10.8 us  [the longest x4 10.8 us: per_device(): earlier.append(lax.ppermute(earlier[-1], ('seq', 'section'), up))]
    ppermute x3, starting transfers between devices: 9.96 us -> 7.33 us  [padded(): lax.ppermute(tail, axis, [(i, (i + 1) % count) for i in range(ends)])]
  transfers between devices with their start and end apart: 6 -> 13, of which waited for: 3 -> 7; matrix products, arithmetic and copies ran while one was open for 1% -> 1% of each run, Pallas kernels for 0% -> 0%
where the time goes in v1:
time: 70.3 us; the launch traced here: 69.9 us
  starting transfers between devices  25.4 us (36%)
  waiting for transfers between devices  22.9 us (33%)
  blocking collectives  8.39 us (12%)
  matrix products  7.84 us (11%)
  local copies, waits for them, and re-layouts  3.02 us (4%)
  other arithmetic  1.38 us (2%)
  between operations  0.99 us (1%)
    ppermute x3, waiting for transfers between devices, padded(): lax.ppermute(head, axis, [((i + 1) % count, i) for i in range(ends)])  12.1 us
    ppermute x3, starting transfers between devices, per_device(): later.append(lax.ppermute(later[-1], ('seq', 'section'), down))  11.8 us
    ppermute x4, waiting for transfers between devices, per_device(): earlier.append(lax.ppermute(earlier[-1], ('seq', 'section'), up))  10.8 us
    ppermute x3, starting transfers between devices, padded(): lax.ppermute(tail, axis, [(i, (i + 1) % count) for i in range(ends)])  7.33 us
    ppermute x3, starting transfers between devices, padded(): lax.ppermute(head, axis, [((i + 1) % count, i) for i in range(ends)])  3.88 us
    dot_general x18, matrix products, pair_conv(): jnp.einsum('co,crs->ors', weight[shift_row, shift_col], window, preferred...  3.11 us
    all_gather x1, blocking collectives, per_device(): full_stem_output = lax.all_gather(stem_own, 'chan', axis=1, tiled=True)  2.49 us
    ppermute x4, starting transfers between devices, per_device(): earlier.append(lax.ppermute(earlier[-1], ('seq', 'section'), up))  2.47 us
  transfers between devices with their start and end apart: 13, of which 7 were waited for; matrix products, arithmetic and copies ran while one was open for 1% of the time, Pallas kernels for 0%

profile of v1, /device:TPU:0, one launch (start us, length us, event | category | flops | bytes accessed | tf_op | source)
XLA Modules:
  0.0 69.9 jit_solution(1659957926643014520)
XLA Ops:
  0.7 1.0 %eq.25 = s32[512,16]{1,0:T(8,128)S(1)} reshape(s32[8192]{0:T(1024)} %param.10) | data formatting | bytes 65536 | tf_op jit(solution)/shard_map/eq | solution.py:76
  1.9 1.2 %convolution_convert_fusion = bf16[512,384]{1,0:T(8,128)(2,1)S(1)} fusion(s32[512,64]{0,1:T(8,128)S(1)} %eq.27, s32[64]{0:T(128)S(1)} %eq.29, bf16[64,768]{1,0:T(8,128)(2,1)} %param.11, s32[]{:T(128)S(6)} %select_n.29), kind=kOutput, calls=%fused_computation.7 | convolution fusion | flops 25395200 | bytes 573700 | tf_op jit(solution)/shard_map/dot_general | solution.py:83
  3.1 2.5 %all_gather.12 = bf16[512,768]{1,0:T(8,128)(2,1)S(1)} all-gather(bf16[512,384]{1,0:T(8,128)(2,1)S(1)} %convolution_convert_fusion), channel_id=1, replica_groups=mesh['groups'=2,'seq'=4,'section'=2,'chan'=2] {'chan'}, dimensions={1}, use_global_device_ids=true | all-gather | bytes 1179648 | tf_op jit(solution)/shard_map/all_gather | solution.py:84
  5.6 4.8 %collective-permute-start = (bf16[4,768]{1,0:T(4,128)(2,1)S(1)}, bf16[4,768]{1,0:T(4,128)(2,1)S(1)}, u32[]{:S(2)}, u32[]{:S(2)}) collective-permute-start(bf16[4,768]{1,0:T(4,128)(2,1)S(1)} %get-tuple-element.4), channel_id=1, source_target_pairs={{0,2},{2,4},{4,6},{6,8},{8,10},{10,12},{12,14},{1,3},{3,5},{5,7},{... | collective-permute-start | bytes 18440 | tf_op jit(solution)/shard_map/ppermute | solution.py:22
  10.4 1.3 %collective-permute-start.1 = (bf16[4,768]{1,0:T(4,128)(2,1)S(1)}, bf16[4,768]{1,0:T(4,128)(2,1)S(1)}, u32[]{:S(2)}, u32[]{:S(2)}) collective-permute-start(bf16[4,768]{1,0:T(4,128)(2,1)S(1)} %get-tuple-element.5), channel_id=1, source_target_pairs={{2,0},{4,2},{6,4},{8,6},{10,8},{12,10},{14,12},{3,1},{5,3},{7,5},{... | collective-permute-start | bytes 18440 | tf_op jit(solution)/shard_map/ppermute | solution.py:24
  11.8 4.1 %collective-permute-done.1 = bf16[4,768]{1,0:T(4,128)(2,1)S(1)} collective-permute-done((bf16[4,768]{1,0:T(4,128)(2,1)S(1)}, bf16[4,768]{1,0:T(4,128)(2,1)S(1)}, u32[]{:S(2)}, u32[]{:S(2)}) %collective-permute-start.1) | collective-permute-done | bytes 6176 | tf_op jit(solution)/shard_map/ppermute | solution.py:24
  19.8 2.1 %all_gather.13 = bf16[256,768]{1,0:T(8,128)(2,1)S(1)} all-gather(bf16[256,384]{1,0:T(8,128)(2,1)S(1)} %max.3), channel_id=1, replica_groups=mesh['groups'=2,'seq'=4,'section'=2,'chan'=2] {'chan'}, dimensions={1}, use_global_device_ids=true | all-gather | bytes 589824 | tf_op jit(solution)/shard_map/all_gather | solution.py:99
  21.9 1.4 %convert_reduce_fusion = (f32[4,768]{1,0:T(4,128)S(1)}, bf16[256,768]{1,0:T(8,128)(2,1)}) fusion(bf16[256,768]{1,0:T(8,128)(2,1)S(1)} %all_gather.13, bf16[768,768]{1,0:T(8,128)(2,1)S(1)} %copy-done), kind=kOutput, calls=%fused_computation.55 | convolution fusion | flops 304149504 | bytes 1978368 | tf_op jit(solution)/shard_map/dot_general | solution.py:98
  23.3 1.8 %all_gather.14 = bf16[4,1536]{1,0:T(4,128)(2,1)S(1)} all-gather(bf16[4,768]{1,0:T(4,128)(2,1)S(1)} %multiply_convert_fusion), channel_id=1, replica_groups=mesh['groups'=2,'seq'=4,'section'=2,'chan'=2] {'chan'}, dimensions={1}, use_global_device_ids=true | all-gather | bytes 18432 | tf_op jit(solution)/shard_map/all_gather | solution.py:108
  25.5 2.5 %collective-permute-start.2 = (bf16[4,256]{1,0:T(4,128)(2,1)S(1)}, bf16[4,256]{1,0:T(4,128)(2,1)S(1)}, u32[]{:S(2)}, u32[]{:S(2)}) collective-permute-start(bf16[4,256]{1,0:T(4,128)(2,1)S(1)} %convolution_convert_fusion.1), channel_id=1, source_target_pairs={{0,2},{2,4},{4,6},{6,8},{8,10},{10,12},{12,14},{14,0},{1,3},{3,5},... | collective-permute-start | bytes 6152 | tf_op jit(solution)/shard_map/ppermute | solution.py:126
  28.0 2.3 %collective-permute-start.6 = (bf16[4,256]{1,0:T(4,128)(2,1)S(1)}, bf16[4,256]{1,0:T(4,128)(2,1)S(1)}, u32[]{:S(2)}, u32[]{:S(2)}) collective-permute-start(bf16[4,256]{1,0:T(4,128)(2,1)S(1)} %convolution_convert_fusion.1), channel_id=1, source_target_pairs={{0,14},{2,0},{4,2},{6,4},{8,6},{10,8},{12,10},{14,12},{1,15},{3,1}... | collective-permute-start | bytes 6152 | tf_op jit(solution)/shard_map/ppermute | solution.py:128
  30.3 1.6 %collective-permute-done.2 = bf16[4,256]{1,0:T(4,128)(2,1)S(1)} collective-permute-done((bf16[4,256]{1,0:T(4,128)(2,1)S(1)}, bf16[4,256]{1,0:T(4,128)(2,1)S(1)}, u32[]{:S(2)}, u32[]{:S(2)}) %collective-permute-start.2) | collective-permute-done | bytes 2080 | tf_op jit(solution)/shard_map/ppermute | solution.py:126
  31.8 4.8 %collective-permute-start.7 = (bf16[4,256]{1,0:T(4,128)(2,1)S(1)}, bf16[4,256]{1,0:T(4,128)(2,1)S(1)}, u32[]{:S(2)}, u32[]{:S(2)}) collective-permute-start(bf16[4,256]{1,0:T(4,128)(2,1)S(1)} %collective-permute-done.6), channel_id=1, source_target_pairs={{0,14},{2,0},{4,2},{6,4},{8,6},{10,8},{12,10},{14,12},{1,15},{3,1}... | collective-permute-start | bytes 6152 | tf_op jit(solution)/shard_map/ppermute | solution.py:128
  36.6 1.5 %collective-permute-done.3 = bf16[4,256]{1,0:T(4,128)(2,1)S(1)} collective-permute-done((bf16[4,256]{1,0:T(4,128)(2,1)S(1)}, bf16[4,256]{1,0:T(4,128)(2,1)S(1)}, u32[]{:S(2)}, u32[]{:S(2)}) %collective-permute-start.3) | collective-permute-done | bytes 2080 | tf_op jit(solution)/shard_map/ppermute | solution.py:126
  38.2 4.7 %collective-permute-start.8 = (bf16[4,256]{1,0:T(4,128)(2,1)S(1)}, bf16[4,256]{1,0:T(4,128)(2,1)S(1)}, u32[]{:S(2)}, u32[]{:S(2)}) collective-permute-start(bf16[4,256]{1,0:T(4,128)(2,1)S(1)} %collective-permute-done.7), channel_id=1, source_target_pairs={{0,14},{2,0},{4,2},{6,4},{8,6},{10,8},{12,10},{14,12},{1,15},{3,1}... | collective-permute-start | bytes 6152 | tf_op jit(solution)/shard_map/ppermute | solution.py:128
  42.9 1.5 %collective-permute-done.4 = bf16[4,256]{1,0:T(4,128)(2,1)S(1)} collective-permute-done((bf16[4,256]{1,0:T(4,128)(2,1)S(1)}, bf16[4,256]{1,0:T(4,128)(2,1)S(1)}, u32[]{:S(2)}, u32[]{:S(2)}) %collective-permute-start.4) | collective-permute-done | bytes 2080 | tf_op jit(solution)/shard_map/ppermute | solution.py:126
  44.4 6.3 %collective-permute-done.5 = bf16[4,256]{1,0:T(4,128)(2,1)S(1)} collective-permute-done((bf16[4,256]{1,0:T(4,128)(2,1)S(1)}, bf16[4,256]{1,0:T(4,128)(2,1)S(1)}, u32[]{:S(2)}, u32[]{:S(2)}) %collective-permute-start.5) | collective-permute-done | bytes 2080 | tf_op jit(solution)/shard_map/ppermute | solution.py:126
  52.6 2.0 %all_gather.15 = bf16[128,8,16]{2,1,0:T(8,128)(2,1)S(1)} all-gather(bf16[64,8,16]{2,1,0:T(8,128)(2,1)S(1)} %copy.17), channel_id=1, replica_groups=mesh['groups'=2,'seq'=4,'section'=2,'chan'=2] {'chan'}, dimensions={0}, use_global_device_ids=true | all-gather | bytes 49152 | tf_op jit(solution)/shard_map/all_gather | solution.py:152
  54.8 1.3 %collective-permute-start.9 = (bf16[128,1,16]{0,2,1:T(8,128)(2,1)S(1)}, bf16[128,1,16]{0,2,1:T(8,128)(2,1)S(1)}, u32[]{:S(2)}, u32[]{:S(2)}) collective-permute-start(bf16[128,1,16]{0,2,1:T(8,128)(2,1)S(1)} %get-tuple-element.10), channel_id=1, source_target_pairs={{0,4},{4,8},{8,12},{1,5},{5,9},{9,13},{2,6},{6,10},{10,14},{3,7},{... | collective-permute-start | bytes 12296 | tf_op jit(solution)/shard_map/ppermute | solution.py:22
  56.1 1.3 %collective-permute-start.10 = (bf16[128,1,16]{0,2,1:T(8,128)(2,1)S(1)}, bf16[128,1,16]{0,2,1:T(8,128)(2,1)S(1)}, u32[]{:S(2)}, u32[]{:S(2)}) collective-permute-start(bf16[128,1,16]{0,2,1:T(8,128)(2,1)S(1)} %get-tuple-element.11), channel_id=1, source_target_pairs={{4,0},{8,4},{12,8},{5,1},{9,5},{13,9},{6,2},{10,6},{14,10},{7,3},{... | collective-permute-start | bytes 12296 | tf_op jit(solution)/shard_map/ppermute | solution.py:24
  57.6 4.0 %collective-permute-done.10 = bf16[128,1,16]{0,2,1:T(8,128)(2,1)S(1)} collective-permute-done((bf16[128,1,16]{0,2,1:T(8,128)(2,1)S(1)}, bf16[128,1,16]{0,2,1:T(8,128)(2,1)S(1)}, u32[]{:S(2)}, u32[]{:S(2)}) %collective-permute-start.10) | collective-permute-done | bytes 4128 | tf_op jit(solution)/shard_map/ppermute | solution.py:24
  61.6 1.3 %collective-permute-start.11 = (bf16[128,10,1]{0,2,1:T(2,128)(2,1)S(1)}, bf16[128,10,1]{0,2,1:T(2,128)(2,1)S(1)}, u32[]{:S(2)}, u32[]{:S(2)}) collective-permute-start(bf16[128,10,1]{0,2,1:T(2,128)(2,1)S(1)} %get-tuple-element.8), channel_id=1, source_target_pairs={{0,2},{1,3},{4,6},{5,7},{8,10},{9,11},{12,14},{13,15},{16,18},{17,... | collective-permute-start | bytes 7688 | tf_op jit(solution)/shard_map/ppermute | solution.py:22
  62.9 1.3 %collective-permute-start.12 = (bf16[128,10,1]{0,2,1:T(2,128)(2,1)S(1)}, bf16[128,10,1]{0,2,1:T(2,128)(2,1)S(1)}, u32[]{:S(2)}, u32[]{:S(2)}) collective-permute-start(bf16[128,10,1]{0,2,1:T(2,128)(2,1)S(1)} %get-tuple-element.9), channel_id=1, source_target_pairs={{2,0},{3,1},{6,4},{7,5},{10,8},{11,9},{14,12},{15,13},{18,16},{19,... | collective-permute-start | bytes 7688 | tf_op jit(solution)/shard_map/ppermute | solution.py:24
  64.5 4.0 %collective-permute-done.12 = bf16[128,10,1]{0,2,1:T(2,128)(2,1)S(1)} collective-permute-done((bf16[128,10,1]{0,2,1:T(2,128)(2,1)S(1)}, bf16[128,10,1]{0,2,1:T(2,128)(2,1)S(1)}, u32[]{:S(2)}, u32[]{:S(2)}) %collective-permute-start.12) | collective-permute-done | bytes 2592 | tf_op jit(solution)/shard_map/ppermute | solution.py:24
  (80 shorter events, 8.7 us)
Async XLA Ops:
  0.6 21.3 %copy-start = (bf16[768,768]{1,0:T(8,128)(2,1)S(1)}, bf16[768,768]{1,0:T(8,128)(2,1)}, u32[]{:S(2)}) copy-start(bf16[768,768]{1,0:T(8,128)(2,1)} %param.14) | copy-start | bytes 3538948
  1.7 14.5 %copy-start.6 = (f32[768]{0:T(1024)S(1)}, f32[768]{0:T(1024)}, u32[]{:S(2)}) copy-start(f32[768]{0:T(1024)} %param.12) | copy-start | bytes 9220
  5.6 6.2 %collective-permute-start = (bf16[4,768]{1,0:T(4,128)(2,1)S(1)}, bf16[4,768]{1,0:T(4,128)(2,1)S(1)}, u32[]{:S(2)}, u32[]{:S(2)}) collective-permute-start(bf16[4,768]{1,0:T(4,128)(2,1)S(1)} %get-tuple-element.4), channel_id=1, source_target_pairs={{0,2},{2,4},{4,6},{6,8},{8,10},{10,12},{12,14},{1,3},{3,5},{5,7},{... | collective-permute-start | bytes 18440 | tf_op jit(solution)/shard_map/ppermute | solution.py:22
  10.4 5.5 %collective-permute-start.1 = (bf16[4,768]{1,0:T(4,128)(2,1)S(1)}, bf16[4,768]{1,0:T(4,128)(2,1)S(1)}, u32[]{:S(2)}, u32[]{:S(2)}) collective-permute-start(bf16[4,768]{1,0:T(4,128)(2,1)S(1)} %get-tuple-element.5), channel_id=1, source_target_pairs={{2,0},{4,2},{6,4},{8,6},{10,8},{12,10},{14,12},{3,1},{5,3},{7,5},{... | collective-permute-start | bytes 18440 | tf_op jit(solution)/shard_map/ppermute | solution.py:24
  11.7 4.9 %copy-start.2 = (bf16[3,768,384]{2,1,0:T(8,128)(2,1)S(1)}, bf16[3,768,384]{2,1,0:T(8,128)(2,1)}, u32[]{:S(2)}) copy-start(bf16[3,768,384]{2,1,0:T(8,128)(2,1)} %param.13) | copy-start | bytes 5308420
  21.9 3.3 %copy-start.1 = (bf16[1536,256]{1,0:T(8,128)(2,1)S(1)}, bf16[1536,256]{1,0:T(8,128)(2,1)}, u32[]{:S(2)}) copy-start(bf16[1536,256]{1,0:T(8,128)(2,1)} %param.16) | copy-start | bytes 2359300
  21.9 3.4 %copy-start.5 = (f32[1536]{0:T(1024)S(1)}, f32[1536]{0:T(1024)}, u32[]{:S(2)}) copy-start(f32[1536]{0:T(1024)} %param.15) | copy-start | bytes 18436
  21.9 29.1 %copy-start.7 = (f32[128]{0:T(128)S(1)}, f32[128]{0:T(128)}, u32[]{:S(2)}) copy-start(f32[128]{0:T(128)} %param.17) | copy-start | bytes 1540
  21.9 29.2 %copy-start.3 = (bf16[3,3,128,64]{2,3,1,0:T(8,128)(2,1)S(1)}, bf16[3,3,128,64]{2,3,1,0:T(8,128)(2,1)}, u32[]{:S(2)}) copy-start(bf16[3,3,128,64]{2,3,1,0:T(8,128)(2,1)} %param.18) | copy-start | bytes 442372
  25.5 31.9 %copy-start.4 = (bf16[3,3,128,64]{2,3,1,0:T(8,128)(2,1)S(1)}, bf16[3,3,128,64]{2,3,1,0:T(8,128)(2,1)}, u32[]{:S(2)}) copy-start(bf16[3,3,128,64]{2,3,1,0:T(8,128)(2,1)} %param.19) | copy-start | bytes 442372
  25.5 6.3 %collective-permute-start.2 = (bf16[4,256]{1,0:T(4,128)(2,1)S(1)}, bf16[4,256]{1,0:T(4,128)(2,1)S(1)}, u32[]{:S(2)}, u32[]{:S(2)}) collective-permute-start(bf16[4,256]{1,0:T(4,128)(2,1)S(1)} %convolution_convert_fusion.1), channel_id=1, source_target_pairs={{0,2},{2,4},{4,6},{6,8},{8,10},{10,12},{12,14},{14,0},{1,3},{3,5},... | collective-permute-start | bytes 6152 | tf_op jit(solution)/shard_map/ppermute | solution.py:126
  28.0 3.8 %collective-permute-start.6 = (bf16[4,256]{1,0:T(4,128)(2,1)S(1)}, bf16[4,256]{1,0:T(4,128)(2,1)S(1)}, u32[]{:S(2)}, u32[]{:S(2)}) collective-permute-start(bf16[4,256]{1,0:T(4,128)(2,1)S(1)} %convolution_convert_fusion.1), channel_id=1, source_target_pairs={{0,14},{2,0},{4,2},{6,4},{8,6},{10,8},{12,10},{14,12},{1,15},{3,1}... | collective-permute-start | bytes 6152 | tf_op jit(solution)/shard_map/ppermute | solution.py:128
  31.8 6.3 %collective-permute-start.3 = (bf16[4,256]{1,0:T(4,128)(2,1)S(1)}, bf16[4,256]{1,0:T(4,128)(2,1)S(1)}, u32[]{:S(2)}, u32[]{:S(2)}) collective-permute-start(bf16[4,256]{1,0:T(4,128)(2,1)S(1)} %collective-permute-done.2), channel_id=1, source_target_pairs={{0,2},{2,4},{4,6},{6,8},{8,10},{10,12},{12,14},{14,0},{1,3},{3,5},... | collective-permute-start | bytes 6152 | tf_op jit(solution)/shard_map/ppermute | solution.py:126
  31.8 6.3 %collective-permute-start.7 = (bf16[4,256]{1,0:T(4,128)(2,1)S(1)}, bf16[4,256]{1,0:T(4,128)(2,1)S(1)}, u32[]{:S(2)}, u32[]{:S(2)}) collective-permute-start(bf16[4,256]{1,0:T(4,128)(2,1)S(1)} %collective-permute-done.6), channel_id=1, source_target_pairs={{0,14},{2,0},{4,2},{6,4},{8,6},{10,8},{12,10},{14,12},{1,15},{3,1}... | collective-permute-start | bytes 6152 | tf_op jit(solution)/shard_map/ppermute | solution.py:128
  38.1 6.3 %collective-permute-start.4 = (bf16[4,256]{1,0:T(4,128)(2,1)S(1)}, bf16[4,256]{1,0:T(4,128)(2,1)S(1)}, u32[]{:S(2)}, u32[]{:S(2)}) collective-permute-start(bf16[4,256]{1,0:T(4,128)(2,1)S(1)} %collective-permute-done.3), channel_id=1, source_target_pairs={{0,2},{2,4},{4,6},{6,8},{8,10},{10,12},{12,14},{14,0},{1,3},{3,5},... | collective-permute-start | bytes 6152 | tf_op jit(solution)/shard_map/ppermute | solution.py:126
  38.2 6.2 %collective-permute-start.8 = (bf16[4,256]{1,0:T(4,128)(2,1)S(1)}, bf16[4,256]{1,0:T(4,128)(2,1)S(1)}, u32[]{:S(2)}, u32[]{:S(2)}) collective-permute-start(bf16[4,256]{1,0:T(4,128)(2,1)S(1)} %collective-permute-done.7), channel_id=1, source_target_pairs={{0,14},{2,0},{4,2},{6,4},{8,6},{10,8},{12,10},{14,12},{1,15},{3,1}... | collective-permute-start | bytes 6152 | tf_op jit(solution)/shard_map/ppermute | solution.py:128
  44.4 6.3 %collective-permute-start.5 = (bf16[4,256]{1,0:T(4,128)(2,1)S(1)}, bf16[4,256]{1,0:T(4,128)(2,1)S(1)}, u32[]{:S(2)}, u32[]{:S(2)}) collective-permute-start(bf16[4,256]{1,0:T(4,128)(2,1)S(1)} %collective-permute-done.4), channel_id=1, source_target_pairs={{0,2},{2,4},{4,6},{6,8},{8,10},{10,12},{12,14},{14,0},{1,3},{3,5},... | collective-permute-start | bytes 6152 | tf_op jit(solution)/shard_map/ppermute | solution.py:126
  54.8 2.8 %collective-permute-start.9 = (bf16[128,1,16]{0,2,1:T(8,128)(2,1)S(1)}, bf16[128,1,16]{0,2,1:T(8,128)(2,1)S(1)}, u32[]{:S(2)}, u32[]{:S(2)}) collective-permute-start(bf16[128,1,16]{0,2,1:T(8,128)(2,1)S(1)} %get-tuple-element.10), channel_id=1, source_target_pairs={{0,4},{4,8},{8,12},{1,5},{5,9},{9,13},{2,6},{6,10},{10,14},{3,7},{... | collective-permute-start | bytes 12296 | tf_op jit(solution)/shard_map/ppermute | solution.py:22
  56.1 5.5 %collective-permute-start.10 = (bf16[128,1,16]{0,2,1:T(8,128)(2,1)S(1)}, bf16[128,1,16]{0,2,1:T(8,128)(2,1)S(1)}, u32[]{:S(2)}, u32[]{:S(2)}) collective-permute-start(bf16[128,1,16]{0,2,1:T(8,128)(2,1)S(1)} %get-tuple-element.11), channel_id=1, source_target_pairs={{4,0},{8,4},{12,8},{5,1},{9,5},{13,9},{6,2},{10,6},{14,10},{7,3},{... | collective-permute-start | bytes 12296 | tf_op jit(solution)/shard_map/ppermute | solution.py:24
  61.6 2.9 %collective-permute-start.11 = (bf16[128,10,1]{0,2,1:T(2,128)(2,1)S(1)}, bf16[128,10,1]{0,2,1:T(2,128)(2,1)S(1)}, u32[]{:S(2)}, u32[]{:S(2)}) collective-permute-start(bf16[128,10,1]{0,2,1:T(2,128)(2,1)S(1)} %get-tuple-element.8), channel_id=1, source_target_pairs={{0,2},{1,3},{4,6},{5,7},{8,10},{9,11},{12,14},{13,15},{16,18},{17,... | collective-permute-start | bytes 7688 | tf_op jit(solution)/shard_map/ppermute | solution.py:22
  62.9 5.5 %collective-permute-start.12 = (bf16[128,10,1]{0,2,1:T(2,128)(2,1)S(1)}, bf16[128,10,1]{0,2,1:T(2,128)(2,1)S(1)}, u32[]{:S(2)}, u32[]{:S(2)}) collective-permute-start(bf16[128,10,1]{0,2,1:T(2,128)(2,1)S(1)} %get-tuple-element.9), channel_id=1, source_target_pairs={{2,0},{3,1},{6,4},{7,5},{10,8},{11,9},{14,12},{15,13},{18,16},{19,... | collective-permute-start | bytes 7688 | tf_op jit(solution)/shard_map/ppermute | solution.py:24
